TPU v7x, 256 devices: a whole 4x4x8 slice. The times are simulated.
256 devices in a mesh: pipe: 8 (over x, z_hi), expert: 32 (over y, z_lo, core).
Axes of the slice: x: 4, y: 4, z: 8 (z_hi: 2, z_lo: 4; z = z_hi * 4 + z_lo), core: 2. Of those that a mesh axis runs over, the one named last changes fastest.
Arguments:
- fwd_acts: bfloat16 [8, 2048, 3584], P('pipe', 'expert'), may hold values from -6 to 6
- fwd_routes: int32 [8, 2048, 2], P('pipe', 'expert'), may hold values from 0 to 7, all different within a row; in each aligned block of 64 rows (0 to 63, 64 to 127, ..., all dimensions but the last counted through in order) at most 20 rows name the same one
- fwd_gates: float32 [8, 2048, 2], P('pipe', 'expert'), may hold values from 0.25 to 1
- back_acts: bfloat16 [8, 2048, 3584], P('pipe', 'expert'), may hold values from -6 to 6
- back_routes: int32 [8, 2048, 2], P('pipe', 'expert'), may hold values from 0 to 7, all different within a row; in each aligned block of 64 rows (0 to 63, 64 to 127, ..., all dimensions but the last counted through in order) at most 20 rows name the same one
- back_gates: float32 [8, 2048, 2], P('pipe', 'expert'), may hold values from 0.25 to 1
- back_grads: bfloat16 [8, 2048, 3584], P('pipe', 'expert'), may hold values from -0.59765625 to 0.59765625
- w_up: bfloat16 [8, 32, 3584, 256], P('pipe', 'expert'), may hold values from -0.09375 to 0.09375
- w_down: bfloat16 [8, 32, 256, 3584], P('pipe', 'expert'), may hold values from -0.1875 to 0.1875
Outputs:
- fwd_next: bfloat16 [8, 2048, 3584], P('pipe', 'expert')
- back_next: bfloat16 [8, 2048, 3584], P('pipe', 'expert')
- grad_up: float32 [8, 32, 3584, 256], P('pipe', 'expert')
- grad_down: float32 [8, 32, 256, 3584], P('pipe', 'expert')
Inputs may be any that keep to these rules, and one draw needn't show every extreme that they name: `fwd_routes`: in each aligned block of 64 rows of a section the 2 experts of a row differ, and each expert is named by at most 20 rows, by exactly 20 in some block. `back_routes`: as for fwd_routes.
All inputs are finite; a program needn't handle non-finite values.
Results may differ from a plain program's by a relative error of at most 0.005.
Values may be sent and summed in bfloat16 or wider, within the bound.
A program may use at most 192 MiB of HBM per device.

v0:
```python
import jax
import jax.numpy as jnp
from jax import lax
from jax.sharding import PartitionSpec as P

GROUP = 4
HIGH = lax.Precision.HIGHEST


def passed_along(value, axis, steps):
    count = lax.axis_size(axis)
    pairs = [(source, (source + steps) % count) for source in range(count)]
    return lax.ppermute(value, axis, pairs)


def silu_grad(value):
    sigma = jax.nn.sigmoid(value)
    return sigma * (1.0 + value * (1.0 - sigma))


def tables(routes, gates, experts, slot_cap):
    tok_rows, top_count = routes.shape
    flat = routes.reshape(tok_rows * top_count)
    onehot = (flat[:, None] == jnp.arange(experts, dtype=jnp.int32)[None, :]).astype(jnp.int32)
    before = jnp.cumsum(onehot, axis=0) - onehot
    slots = jnp.sum(before * onehot, axis=1)
    places = flat * slot_cap + slots
    columns = jnp.arange(experts * slot_cap, dtype=jnp.int32)
    hits = (
        (places[:, None] == columns[None, :])
        .astype(jnp.float32)
        .reshape(tok_rows, top_count, experts * slot_cap)
    )
    plain = jnp.sum(hits, axis=1)
    gated = jnp.sum(hits * gates[:, :, None], axis=1)
    return (plain, gated)


def gather_rows(plain, values):
    return lax.dot_general(
        plain.astype(jnp.bfloat16),
        values,
        (((0,), (0,)), ((), ())),
        preferred_element_type=jnp.float32,
    ).astype(jnp.bfloat16)


def send_rows(stacked, experts, slot_cap):
    count, _, model_width = stacked.shape
    copies = jnp.repeat(stacked.reshape(count, experts, 1, slot_cap, model_width), GROUP, axis=2)
    copies = copies.reshape(count, experts * GROUP, slot_cap, model_width)
    received = lax.all_to_all(copies, "expert", split_axis=1, concat_axis=1, tiled=True)
    return received.reshape(count, -1, model_width)


def send_back(parts, experts, slot_cap):
    count, _, model_width = parts.shape
    arranged = parts.reshape(count, experts * GROUP, slot_cap, model_width)
    received = lax.all_to_all(arranged, "expert", split_axis=1, concat_axis=1, tiled=True)
    summed = jnp.sum(
        received.reshape(count, experts, GROUP, slot_cap, model_width), axis=2, dtype=jnp.float32
    )
    return summed.reshape(count, experts * slot_cap, model_width)


def expert_forward(rows, up_proj, down_proj):
    pre = jnp.dot(rows, up_proj, preferred_element_type=jnp.float32)
    act = jax.nn.silu(pre).astype(jnp.bfloat16)
    return jnp.dot(act, down_proj, preferred_element_type=jnp.float32).astype(jnp.bfloat16)


def expert_backward(rows, grad_rows, up_proj, down_proj):
    pre = jnp.dot(rows, up_proj, preferred_element_type=jnp.float32)
    act = jax.nn.silu(pre).astype(jnp.bfloat16)
    dact = lax.dot_general(
        grad_rows, down_proj, (((1,), (1,)), ((), ())), preferred_element_type=jnp.float32
    )
    dpre = (dact * silu_grad(pre)).astype(jnp.bfloat16)
    dpart = lax.dot_general(
        dpre, up_proj, (((1,), (1,)), ((), ())), preferred_element_type=jnp.float32
    ).astype(jnp.bfloat16)
    grad_up = lax.dot_general(
        rows, dpre, (((0,), (0,)), ((), ())), preferred_element_type=jnp.float32
    )
    grad_down = lax.dot_general(
        act, grad_rows, (((0,), (0,)), ((), ())), preferred_element_type=jnp.float32
    )
    return (dpart, grad_up, grad_down)


def local(
    fwd_acts, fwd_routes, fwd_gates, back_acts, back_routes, back_gates, back_grads, w_up, w_down
):
    devices = lax.axis_size("expert")
    experts = devices // GROUP
    tok_rows = fwd_acts.shape[1]
    top_count = fwd_routes.shape[2]
    slot_cap = GROUP * (5 * tok_rows * top_count // (4 * devices))
    up_proj = w_up[0, 0]
    down_proj = w_down[0, 0]
    fwd_input = fwd_acts[0]
    back_input = back_acts[0]
    out_grad = back_grads[0]
    plain_f, gated_f = tables(fwd_routes[0], fwd_gates[0], experts, slot_cap)
    plain_b, gated_b = tables(back_routes[0], back_gates[0], experts, slot_cap)
    buffer_f = gather_rows(plain_f, fwd_input)
    buffer_x = gather_rows(plain_b, back_input)
    buffer_g = lax.dot_general(
        gated_b, out_grad.astype(jnp.float32), (((0,), (0,)), ((), ())), precision=HIGH
    ).astype(jnp.bfloat16)
    got_f = send_rows(buffer_f[None], experts, slot_cap)
    part = expert_forward(got_f[0], up_proj, down_proj)
    summed_f = send_back(part[None], experts, slot_cap)[0]
    got_b = send_rows(jnp.stack([buffer_x, buffer_g]), experts, slot_cap)
    dpart, grad_up, grad_down = expert_backward(got_b[0], got_b[1], up_proj, down_proj)
    summed_b = send_back(dpart[None], experts, slot_cap)[0]
    merged = jnp.dot(gated_f, summed_f, precision=HIGH)
    section_out = (fwd_input.astype(jnp.float32) + merged).astype(jnp.bfloat16)
    spread_back = jnp.dot(plain_b, summed_b, precision=HIGH)
    section_grad = (out_grad.astype(jnp.float32) + spread_back).astype(jnp.bfloat16)
    fwd_next = passed_along(section_out[None], "pipe", 1)
    back_next = passed_along(section_grad[None], "pipe", -1)
    return (fwd_next, back_next, grad_up[None, None], grad_down[None, None])


def solution(mesh):
    in_specs = (
        P("pipe", "expert", None),
        P("pipe", "expert", None),
        P("pipe", "expert", None),
        P("pipe", "expert", None),
        P("pipe", "expert", None),
        P("pipe", "expert", None),
        P("pipe", "expert", None),
        P("pipe", "expert", None, None),
        P("pipe", "expert", None, None),
    )
    out_specs = (
        P("pipe", "expert", None),
        P("pipe", "expert", None),
        P("pipe", "expert", None, None),
        P("pipe", "expert", None, None),
    )
    return jax.shard_map(local, mesh=mesh, in_specs=in_specs, out_specs=out_specs, check_vma=False)
```

profile of v0, /device:TPU:6, one launch (start us, length us, event | category | flops | bytes accessed | tf_op | source)
XLA Modules:
  0.0 673.3 jit_solution(2642117069289322087)
XLA Ops:
  0.6 0.0 copy-start
  0.6 0.9 copy.40
  1.5 0.1 eq.58
  1.7 0.1 fusion.28
  1.8 0.2 reduce_window_sum.17
  2.0 0.2 select_reduce_fusion.3
  2.1 0.1 reduce_sum.77
  2.3 0.1 copy.41
  2.4 0.7 bitcast_add_fusion.1
  3.1 0.8 convert_reduce_fusion.3
  3.8 2.5 convolution_convert_fusion.4
  6.3 1.4 reshape_broadcast_in_dim.9
  7.7 2.9 broadcast_in_dim.26
  10.6 9.2 %all-to-all-start = ((bf16[1,32,20,3584]{3,2,0,1:T(8,128)(2,1)}), bf16[1,32,20,3584]{3,2,0,1:T(8,128)(2,1)}, u32[]{:S(2)}, u32[]{:S(2)}) async-start(bf16[1,32,20,3584]{3,2,0,1:T(8,128)(2,1)} %bitcast.71), calls=%async_computation | async-start | bytes 11010048 | tf_op jit(solution)/shard_map/all_to_all | solution.py:52
  19.8 0.0 copy-done.5
  19.8 0.1 copy.43
  19.9 0.1 eq.65
  20.0 0.1 fusion.27
  20.1 0.2 reduce_window_sum.18
  20.3 0.2 select_reduce_fusion.2
  20.5 0.1 reduce_sum.82
  20.6 0.1 copy.44
  20.7 0.0 copy-done.6
  20.7 0.1 select_reduce_fusion
  20.8 0.0 copy-done.4
  20.8 1.5 convolution_convert_fusion.3
  22.3 1.4 stack.9
  23.7 3.1 convolution_convert_fusion.2
  26.8 2.3 stack.10
  29.1 1.7 maximum_bitcast_fusion
  30.7 3.7 copy.45
  34.5 108.8 %all-to-all-done = bf16[1,32,20,3584]{3,2,0,1:T(8,128)(2,1)} async-done(((bf16[1,32,20,3584]{3,2,0,1:T(8,128)(2,1)}), bf16[1,32,20,3584]{3,2,0,1:T(8,128)(2,1)}, u32[]{:S(2)}, u32[]{:S(2)}) %all-to-all-start) | async-done | bytes 4587552 | tf_op jit(solution)/shard_map/all_to_all | solution.py:52
  143.3 7.1 %broadcast_in_dim.29 = bf16[2,8,1,4,20,3584]{5,0,4,3,1,2:T(2,128)(2,1)} broadcast(bf16[2,8,20,3584]{3,0,2,1:T(2,128)(2,1)} %copy.45), dimensions={0,1,4,5} | broadcast | bytes 11468800 | tf_op jit(solution)/shard_map/broadcast_in_dim | solution.py:50
  150.4 5.0 all-to-all-start.2
  155.3 7.3 %squeeze_reshape.9 = bf16[640,3584]{1,0:T(8,128)(2,1)} reshape(bf16[1,32,20,3584]{3,2,0,1:T(8,128)(2,1)} %all-to-all-done) | data formatting | bytes 9175040 | tf_op jit(solution)/shard_map/squeeze;reshape | solution.py:112
  162.6 9.8 %convolution_convert_fusion.1 = bf16[640,3584]{1,0:T(8,128)(2,1)} fusion(bf16[1,1,256,3584]{3,2,1,0:T(8,128)(2,1)} %param.17, bf16[640,3584]{1,0:T(8,128)(2,1)} %squeeze_reshape.9, bf16[1,1,3584,256]{3,2,1,0:T(8,128)(2,1)S(1)} %copy-done), kind=kOutput, calls=%fused_computation.5 | convolution fusion | flops 2351923200 | bytes 12845056 | tf_op jit(solution)/shard_map/dot_general | solution.py:69
  172.5 7.2 %reshape_broadcast_in_dim.10 = bf16[1,32,20,3584]{3,2,1,0:T(8,128)(2,1)} reshape(bf16[640,3584]{1,0:T(8,128)(2,1)} %convolution_convert_fusion.1) | data formatting | bytes 9175040 | tf_op jit(solution)/shard_map/reshape;broadcast_in_dim | solution.py:58
  179.7 177.8 %all-to-all-done.2 = bf16[2,32,20,3584]{3,0,2,1:T(2,128)(2,1)} async-done(((bf16[2,32,20,3584]{3,0,2,1:T(2,128)(2,1)}), bf16[2,32,20,3584]{3,0,2,1:T(2,128)(2,1)}, u32[]{:S(2)}, u32[]{:S(2)}) %all-to-all-start.2) | async-done | bytes 9175072 | tf_op jit(solution)/shard_map/all_to_all | solution.py:52
  357.5 5.1 all-to-all-start.1
  362.6 45.7 %slice_reduce_fusion = (bf16[32,20,3584]{2,1,0:T(8,128)(2,1)}, bf16[32,20,3584]{2,1,0:T(8,128)(2,1)}) fusion(bf16[2,32,20,3584]{3,0,2,1:T(2,128)(2,1)} %all-to-all-done.2), kind=kLoop, calls=%fused_computation.2 | loop fusion | bytes 18350080 | tf_op jit(solution)/shard_map/slice | solution.py:115
  408.3 7.3 %squeeze.27 = bf16[640,3584]{1,0:T(8,128)(2,1)} reshape(bf16[32,20,3584]{2,1,0:T(8,128)(2,1)} %get-tuple-element.4) | data formatting | bytes 9175040 | tf_op jit(solution)/shard_map/squeeze | solution.py:115
  415.6 7.3 %squeeze.26 = bf16[640,3584]{1,0:T(8,128)(2,1)} reshape(bf16[32,20,3584]{2,1,0:T(8,128)(2,1)} %get-tuple-element.5) | data formatting | bytes 9175040 | tf_op jit(solution)/shard_map/squeeze | solution.py:115
  422.8 3.8 fusion.8
  426.6 0.5 copy-done.7
  427.1 1.4 fusion.15
  428.5 3.6 convolution_convert_fusion
  432.1 7.3 %reshape_broadcast_in_dim.11 = bf16[1,32,20,3584]{3,2,1,0:T(8,128)(2,1)} reshape(bf16[640,3584]{1,0:T(8,128)(2,1)} %convolution_convert_fusion) | data formatting | bytes 9175040 | tf_op jit(solution)/shard_map/reshape;broadcast_in_dim | solution.py:58
  439.3 46.5 %all-to-all-done.1 = bf16[1,32,20,3584]{3,2,0,1:T(8,128)(2,1)} async-done(((bf16[1,32,20,3584]{3,2,0,1:T(8,128)(2,1)}), bf16[1,32,20,3584]{3,2,0,1:T(8,128)(2,1)}, u32[]{:S(2)}, u32[]{:S(2)}) %all-to-all-start.1) | async-done | bytes 4587552 | tf_op jit(solution)/shard_map/all_to_all | solution.py:59
  485.9 4.9 all-to-all-start.3
  490.8 5.3 convert_reduce_fusion.1
  496.0 2.9 squeeze_reshape.10
  499.0 3.7 fusion.3
  502.7 4.5 collective-permute-start
  507.2 5.8 convolution_bitcast_fusion.1
  513.0 120.9 %all-to-all-done.3 = bf16[1,32,20,3584]{3,2,0,1:T(8,128)(2,1)} async-done(((bf16[1,32,20,3584]{3,2,0,1:T(8,128)(2,1)}), bf16[1,32,20,3584]{3,2,0,1:T(8,128)(2,1)}, u32[]{:S(2)}, u32[]{:S(2)}) %all-to-all-start.3) | async-done | bytes 4587552 | tf_op jit(solution)/shard_map/all_to_all | solution.py:59
  633.9 5.3 convert_reduce_fusion
  639.2 2.9 squeeze_reshape.11
  642.1 3.0 fusion.2
  645.1 4.8 collective-permute-start.1
  649.9 5.8 convolution_bitcast_fusion
  655.7 0.0 collective-permute-done
  655.7 15.0 %collective-permute-done.1 = bf16[1,64,3584]{2,1,0:T(8,128)(2,1)S(1)} collective-permute-done((bf16[1,64,3584]{2,1,0:T(8,128)(2,1)S(1)}, bf16[1,64,3584]{2,1,0:T(8,128)(2,1)S(1)}, u32[]{:S(2)}, u32[]{:S(2)}) %collective-permute-start.1) | collective-permute-done | bytes 458784 | tf_op jit(solution)/shard_map/ppermute | solution.py:13
  670.7 1.8 copy.51
  672.5 0.8 copy.52
  (12 shorter events, 0.0 us)
Async XLA Ops:
  0.6 162.0 %copy-start = (bf16[1,1,3584,256]{3,2,1,0:T(8,128)(2,1)S(1)}, bf16[1,1,3584,256]{3,2,1,0:T(8,128)(2,1)}, u32[]{:S(2)}) copy-start(bf16[1,1,3584,256]{3,2,1,0:T(8,128)(2,1)} %param.16) | copy-start | bytes 5505028
  10.6 9.2 %copy-start.5 = (s32[1,64,2]{1,2,0:T(2,128)S(1)}, s32[1,64,2]{1,2,0:T(2,128)}, u32[]{:S(2)}) copy-start(s32[1,64,2]{1,2,0:T(2,128)} %param.13) | copy-start | bytes 1540
  10.6 10.1 %copy-start.6 = (f32[1,64,2]{1,2,0:T(2,128)S(1)}, f32[1,64,2]{1,2,0:T(2,128)}, u32[]{:S(2)}) copy-start(f32[1,64,2]{1,2,0:T(2,128)} %param.14) | copy-start | bytes 1540
  10.6 10.2 %copy-start.4 = (bf16[1,64,3584]{2,1,0:T(8,128)(2,1)S(1)}, bf16[1,64,3584]{2,1,0:T(8,128)(2,1)}, u32[]{:S(2)}) copy-start(bf16[1,64,3584]{2,1,0:T(8,128)(2,1)} %param.12) | copy-start | bytes 1376260
  10.6 132.7 %all-to-all-start = ((bf16[1,32,20,3584]{3,2,0,1:T(8,128)(2,1)}), bf16[1,32,20,3584]{3,2,0,1:T(8,128)(2,1)}, u32[]{:S(2)}, u32[]{:S(2)}) async-start(bf16[1,32,20,3584]{3,2,0,1:T(8,128)(2,1)} %bitcast.71), calls=%async_computation | async-start | bytes 11010048 | tf_op jit(solution)/shard_map/all_to_all | solution.py:52
  150.4 207.1 %all-to-all-start.2 = ((bf16[2,32,20,3584]{3,0,2,1:T(2,128)(2,1)}), bf16[2,32,20,3584]{3,0,2,1:T(2,128)(2,1)}, u32[]{:S(2)}, u32[]{:S(2)}) async-start(bf16[2,32,20,3584]{3,0,2,1:T(2,128)(2,1)} %bitcast.70), calls=%async_computation.2 | async-start | bytes 18350080 | tf_op jit(solution)/shard_map/all_to_all | solution.py:52
  357.5 128.4 %all-to-all-start.1 = ((bf16[1,32,20,3584]{3,2,0,1:T(8,128)(2,1)}), bf16[1,32,20,3584]{3,2,0,1:T(8,128)(2,1)}, u32[]{:S(2)}, u32[]{:S(2)}) async-start(bf16[1,32,20,3584]{3,2,0,1:T(8,128)(2,1)} %bitcast.73), calls=%async_computation.1 | async-start | bytes 11010048 | tf_op jit(solution)/shard_map/all_to_all | solution.py:59
  422.8 3.8 copy-start.1
  422.8 4.3 copy-start.7
  485.9 148.0 %all-to-all-start.3 = ((bf16[1,32,20,3584]{3,2,0,1:T(8,128)(2,1)}), bf16[1,32,20,3584]{3,2,0,1:T(8,128)(2,1)}, u32[]{:S(2)}, u32[]{:S(2)}) async-start(bf16[1,32,20,3584]{3,2,0,1:T(8,128)(2,1)} %bitcast.72), calls=%async_computation.3 | async-start | bytes 11010048 | tf_op jit(solution)/shard_map/all_to_all | solution.py:59
  496.0 2.9 copy-start.2
  502.7 153.0 %collective-permute-start = (bf16[1,64,3584]{2,1,0:T(8,128)(2,1)}, bf16[1,64,3584]{2,1,0:T(8,128)(2,1)}, u32[]{:S(2)}, u32[]{:S(2)}) collective-permute-start(bf16[1,64,3584]{2,1,0:T(8,128)(2,1)} %fusion.3), channel_id=1, source_target_pairs={{0,32},{32,64},{64,96},{96,128},{128,160},{160,192},{192,224},{224... | collective-permute-start | bytes 1376264 | tf_op jit(solution)/shard_map/ppermute | solution.py:13
  639.2 2.9 copy-start.3
  645.1 25.6 %collective-permute-start.1 = (bf16[1,64,3584]{2,1,0:T(8,128)(2,1)S(1)}, bf16[1,64,3584]{2,1,0:T(8,128)(2,1)S(1)}, u32[]{:S(2)}, u32[]{:S(2)}) collective-permute-start(bf16[1,64,3584]{2,1,0:T(8,128)(2,1)S(1)} %fusion.2), channel_id=1, source_target_pairs={{0,224},{32,0},{64,32},{96,64},{128,96},{160,128},{192,160},{224,1... | collective-permute-start | bytes 1376264 | tf_op jit(solution)/shard_map/ppermute | solution.py:13
where the time goes:
time: 675 us; the launch traced here: 673 us
  waiting for transfers between devices  469 us (69%)
  local copies, waits for them, and re-layouts  111 us (16%)
  matrix products  43.9 us (7%)
  starting transfers between devices  33.4 us (5%)
  other arithmetic  14.7 us (2%)
    all_to_all x2, waiting for transfers between devices, send_rows(): lax.all_to_all(copies, 'expert', split_axis=1, concat_axis=1, tiled=True)  287 us
    all_to_all x2, waiting for transfers between devices, send_back(): lax.all_to_all(arranged, 'expert', split_axis=1, concat_axis=1, tiled=True)  167 us
    slice x1, local copies, waits for them, and re-layouts, local(): got_b[0]  45.7 us
    ppermute x2, waiting for transfers between devices, passed_along(): return lax.ppermute(value, axis, pairs)  15 us
    another operation x2, local copies, waits for them, and re-layouts, send_back(): arranged = parts.reshape(count, experts * GROUP, slot_cap, model_width)  14.5 us
    all_to_all x2, starting transfers between devices, send_rows(): lax.all_to_all(copies, 'expert', split_axis=1, concat_axis=1, tiled=True)  14.2 us
  transfers between devices with their start and end apart: 6, of which 5 were waited for; matrix products, arithmetic and copies ran while one was open for 22% of the time, Pallas kernels for 0%

commit v1 on v0

--- a/solution.py
+++ b/solution.py
@@ -49,7 +49,12 @@
     count, _, model_width = stacked.shape
     copies = jnp.repeat(stacked.reshape(count, experts, 1, slot_cap, model_width), GROUP, axis=2)
     copies = copies.reshape(count, experts * GROUP, slot_cap, model_width)
-    received = lax.all_to_all(copies, "expert", split_axis=1, concat_axis=1, tiled=True)
+    received = jnp.concatenate(
+        lax.all_to_all(
+            jnp.stack(jnp.split(copies, lax.axis_size("expert"), axis=1)), "expert", 0, 0
+        ),
+        axis=1,
+    )
     return received.reshape(count, -1, model_width)
 
 

time: 675 us -> 693 us (1.027)
  local copies, waits for them, and re-layouts: 111 us -> 157 us
  waiting for transfers between devices: 469 us -> 436 us
    unnamed x20 -> x82, local copies, waits for them, and re-layouts: 4.07 us -> 53.5 us
    all_to_all x2, waiting for transfers between devices: 287 us -> 253 us  [send_rows(): lax.all_to_all(jnp.stack(jnp.split(copies, lax.axis_size('expert'), axis=...]
  transfers between devices with their start and end apart: 6 -> 6, of which waited for: 5 -> 5; matrix products, arithmetic and copies ran while one was open for 22% -> 27% of each run, Pallas kernels for 0% -> 0%
where the time goes in v1:
time: 693 us; the launch traced here: 686 us
  waiting for transfers between devices  436 us (63%)
  local copies, waits for them, and re-layouts  157 us (23%)
  matrix products  44 us (6%)
  starting transfers between devices  33.6 us (5%)
  other arithmetic  14.7 us (2%)
    all_to_all x2, waiting for transfers between devices, send_rows(): lax.all_to_all(jnp.stack(jnp.split(copies, lax.axis_size('expert'), axis=...  253 us
    all_to_all x2, waiting for transfers between devices, send_back(): lax.all_to_all(arranged, 'expert', split_axis=1, concat_axis=1, tiled=True)  168 us
    unnamed x82, local copies, waits for them, and re-layouts  53.5 us
    slice x1, local copies, waits for them, and re-layouts, local(): got_b[0]  45.5 us
    ppermute x2, waiting for transfers between devices, passed_along(): return lax.ppermute(value, axis, pairs)  15 us
    another operation x2, local copies, waits for them, and re-layouts, send_back(): arranged = parts.reshape(count, experts * GROUP, slot_cap, model_width)  14.4 us
    all_to_all x2, starting transfers between devices, send_rows(): lax.all_to_all(jnp.stack(jnp.split(copies, lax.axis_size('expert'), axis=...  14.1 us
  transfers between devices with their start and end apart: 6, of which 5 were waited for; matrix products, arithmetic and copies ran while one was open for 27% of the time, Pallas kernels for 0%

profile of v1, /device:TPU:6, one launch (start us, length us, event | category | flops | bytes accessed | tf_op | source)
XLA Modules:
  0.0 685.9 jit_solution(16961208745814352707)
XLA Ops:
  0.6 0.9 copy.134
  3.8 2.5 convolution_convert_fusion.4
  6.3 1.4 reshape_broadcast_in_dim.9
  29.9 9.2 %all-to-all-start = ((bf16[32,1,1,20,3584]{4,3,2,1,0:T(8,128)(2,1)}), bf16[32,1,1,20,3584]{4,3,2,1,0:T(8,128)(2,1)}, u32[]{:S(2)}, u32[]{:S(2)}) async-start(bf16[32,1,1,20,3584]{4,3,2,1,0:T(8,128)(2,1)} %fusion.59), calls=%async_computation | async-start | bytes 11010048 | tf_op jit(solution)/shard_map/all_to_all | solution.py:53
  40.2 1.5 convolution_convert_fusion.3
  41.6 1.4 stack.240
  43.0 3.1 convolution_convert_fusion.2
  46.1 2.3 stack.241
  48.4 1.7 maximum_bitcast_fusion
  50.1 2.4 copy.139
  52.4 5.6 broadcast_in_dim.29
  58.1 0.9 fusion.58
  60.8 0.9 fusion.55
  61.7 0.9 fusion.54
  62.6 0.9 fusion.53
  63.5 0.9 fusion.52
  64.4 0.9 fusion.51
  67.1 0.9 fusion.48
  68.1 0.9 fusion.47
  69.0 0.9 fusion.46
  69.9 0.9 fusion.45
  70.8 1.0 fusion.44
  71.8 0.9 fusion.43
  73.6 0.9 fusion.41
  74.5 0.9 fusion.40
  75.4 0.9 fusion.39
  76.3 0.9 fusion.38
  77.3 0.9 fusion.37
  78.2 0.9 fusion.36
  79.1 0.9 fusion.35
  81.8 0.9 fusion.32
  82.7 0.9 fusion.31
  83.6 0.9 fusion.30
  85.5 0.9 fusion.28
  86.4 0.9 fusion.27
  87.3 75.3 %all-to-all-done = bf16[32,1,1,20,3584]{4,3,2,1,0:T(8,128)(2,1)} async-done(((bf16[32,1,1,20,3584]{4,3,2,1,0:T(8,128)(2,1)}), bf16[32,1,1,20,3584]{4,3,2,1,0:T(8,128)(2,1)}, u32[]{:S(2)}, u32[]{:S(2)}) %all-to-all-start) | async-done | bytes 4587552 | tf_op jit(solution)/shard_map/all_to_all | solution.py:53
  162.6 5.0 all-to-all-start.2
  167.6 7.3 %squeeze_reshape_reshape.3 = bf16[640,3584]{1,0:T(8,128)(2,1)} reshape(bf16[32,1,1,20,3584]{4,3,2,1,0:T(8,128)(2,1)} %all-to-all-done) | data formatting | bytes 9175040 | tf_op jit(solution)/shard_map/squeeze;reshape;reshape | solution.py:117
  174.9 9.9 %convolution_convert_fusion.1 = bf16[640,3584]{1,0:T(8,128)(2,1)} fusion(bf16[1,1,256,3584]{3,2,1,0:T(8,128)(2,1)} %param.17, bf16[640,3584]{1,0:T(8,128)(2,1)} %squeeze_reshape_reshape.3, bf16[1,1,3584,256]{3,2,1,0:T(8,128)(2,1)S(1)} %copy-done), kind=kOutput, calls=%fused_computation.5 | convolution fusion | flops 2351923200 | bytes 12845056 | tf_op jit(solution)/shard_map/dot_general | solution.py:74
  184.8 7.2 %reshape_broadcast_in_dim.10 = bf16[1,32,20,3584]{3,2,1,0:T(8,128)(2,1)} reshape(bf16[640,3584]{1,0:T(8,128)(2,1)} %convolution_convert_fusion.1) | data formatting | bytes 9175040 | tf_op jit(solution)/shard_map/reshape;broadcast_in_dim | solution.py:63
  192.0 177.8 %all-to-all-done.2 = bf16[32,2,1,20,3584]{4,1,3,2,0:T(2,128)(2,1)} async-done(((bf16[32,2,1,20,3584]{4,1,3,2,0:T(2,128)(2,1)}), bf16[32,2,1,20,3584]{4,1,3,2,0:T(2,128)(2,1)}, u32[]{:S(2)}, u32[]{:S(2)}) %all-to-all-start.2) | async-done | bytes 9175072 | tf_op jit(solution)/shard_map/all_to_all | solution.py:53
  369.7 5.1 all-to-all-start.1
  374.8 45.5 %slice_reduce_fusion = (bf16[32,20,3584]{2,1,0:T(8,128)(2,1)}, bf16[32,20,3584]{2,1,0:T(8,128)(2,1)}) fusion(bf16[2,32,1,20,3584]{4,0,3,2,1:T(2,128)(2,1)} %bitcast.79), kind=kLoop, calls=%fused_computation.2 | loop fusion | bytes 18350080 | tf_op jit(solution)/shard_map/slice | solution.py:120
  420.2 7.3 %squeeze.27 = bf16[640,3584]{1,0:T(8,128)(2,1)} reshape(bf16[32,20,3584]{2,1,0:T(8,128)(2,1)} %get-tuple-element.4) | data formatting | bytes 9175040 | tf_op jit(solution)/shard_map/squeeze | solution.py:120
  427.5 7.3 %squeeze.26 = bf16[640,3584]{1,0:T(8,128)(2,1)} reshape(bf16[32,20,3584]{2,1,0:T(8,128)(2,1)} %get-tuple-element.5) | data formatting | bytes 9175040 | tf_op jit(solution)/shard_map/squeeze | solution.py:120
  434.8 3.8 fusion.8
  439.1 1.4 fusion.15
  440.5 3.6 convolution_convert_fusion
  444.1 7.2 %reshape_broadcast_in_dim.11 = bf16[1,32,20,3584]{3,2,1,0:T(8,128)(2,1)} reshape(bf16[640,3584]{1,0:T(8,128)(2,1)} %convolution_convert_fusion) | data formatting | bytes 9175040 | tf_op jit(solution)/shard_map/reshape;broadcast_in_dim | solution.py:63
  451.3 47.0 %all-to-all-done.1 = bf16[1,32,20,3584]{3,2,0,1:T(8,128)(2,1)} async-done(((bf16[1,32,20,3584]{3,2,0,1:T(8,128)(2,1)}), bf16[1,32,20,3584]{3,2,0,1:T(8,128)(2,1)}, u32[]{:S(2)}, u32[]{:S(2)}) %all-to-all-start.1) | async-done | bytes 4587552 | tf_op jit(solution)/shard_map/all_to_all | solution.py:64
  498.3 4.9 all-to-all-start.3
  503.2 5.3 convert_reduce_fusion.1
  508.4 2.9 squeeze_reshape.6
  511.3 3.7 fusion.3
  515.0 4.7 collective-permute-start
  519.8 5.8 convolution_bitcast_fusion.1
  525.6 120.7 %all-to-all-done.3 = bf16[1,32,20,3584]{3,2,0,1:T(8,128)(2,1)} async-done(((bf16[1,32,20,3584]{3,2,0,1:T(8,128)(2,1)}), bf16[1,32,20,3584]{3,2,0,1:T(8,128)(2,1)}, u32[]{:S(2)}, u32[]{:S(2)}) %all-to-all-start.3) | async-done | bytes 4587552 | tf_op jit(solution)/shard_map/all_to_all | solution.py:64
  646.3 5.3 convert_reduce_fusion
  651.6 2.9 squeeze_reshape.7
  654.5 3.0 fusion.2
  657.5 4.8 collective-permute-start.1
  662.3 5.8 convolution_bitcast_fusion
  668.0 15.0 %collective-permute-done.1 = bf16[1,64,3584]{2,1,0:T(8,128)(2,1)S(1)} collective-permute-done((bf16[1,64,3584]{2,1,0:T(8,128)(2,1)S(1)}, bf16[1,64,3584]{2,1,0:T(8,128)(2,1)S(1)}, u32[]{:S(2)}, u32[]{:S(2)}) %collective-permute-start.1) | collective-permute-done | bytes 458784 | tf_op jit(solution)/shard_map/ppermute | solution.py:13
  683.0 1.8 copy.207
  (76 shorter events, 33.9 us)
Async XLA Ops:
  0.6 174.3 %copy-start = (bf16[1,1,3584,256]{3,2,1,0:T(8,128)(2,1)S(1)}, bf16[1,1,3584,256]{3,2,1,0:T(8,128)(2,1)}, u32[]{:S(2)}) copy-start(bf16[1,1,3584,256]{3,2,1,0:T(8,128)(2,1)} %param.16) | copy-start | bytes 5505028
  29.9 9.2 %copy-start.5 = (s32[1,64,2]{1,2,0:T(2,128)S(1)}, s32[1,64,2]{1,2,0:T(2,128)}, u32[]{:S(2)}) copy-start(s32[1,64,2]{1,2,0:T(2,128)} %param.13) | copy-start | bytes 1540
  29.9 10.1 %copy-start.6 = (f32[1,64,2]{1,2,0:T(2,128)S(1)}, f32[1,64,2]{1,2,0:T(2,128)}, u32[]{:S(2)}) copy-start(f32[1,64,2]{1,2,0:T(2,128)} %param.14) | copy-start | bytes 1540
  29.9 10.2 %copy-start.4 = (bf16[1,64,3584]{2,1,0:T(8,128)(2,1)S(1)}, bf16[1,64,3584]{2,1,0:T(8,128)(2,1)}, u32[]{:S(2)}) copy-start(bf16[1,64,3584]{2,1,0:T(8,128)(2,1)} %param.12) | copy-start | bytes 1376260
  29.9 132.7 %all-to-all-start = ((bf16[32,1,1,20,3584]{4,3,2,1,0:T(8,128)(2,1)}), bf16[32,1,1,20,3584]{4,3,2,1,0:T(8,128)(2,1)}, u32[]{:S(2)}, u32[]{:S(2)}) async-start(bf16[32,1,1,20,3584]{4,3,2,1,0:T(8,128)(2,1)} %fusion.59), calls=%async_computation | async-start | bytes 11010048 | tf_op jit(solution)/shard_map/all_to_all | solution.py:53
  162.6 207.1 %all-to-all-start.2 = ((bf16[32,2,1,20,3584]{4,1,3,2,0:T(2,128)(2,1)}), bf16[32,2,1,20,3584]{4,1,3,2,0:T(2,128)(2,1)}, u32[]{:S(2)}, u32[]{:S(2)}) async-start(bf16[32,2,1,20,3584]{4,1,3,2,0:T(2,128)(2,1)} %fusion.27), calls=%async_computation.2 | async-start | bytes 18350080 | tf_op jit(solution)/shard_map/all_to_all | solution.py:53
  369.7 128.5 %all-to-all-start.1 = ((bf16[1,32,20,3584]{3,2,0,1:T(8,128)(2,1)}), bf16[1,32,20,3584]{3,2,0,1:T(8,128)(2,1)}, u32[]{:S(2)}, u32[]{:S(2)}) async-start(bf16[1,32,20,3584]{3,2,0,1:T(8,128)(2,1)} %bitcast.390), calls=%async_computation.1 | async-start | bytes 11010048 | tf_op jit(solution)/shard_map/all_to_all | solution.py:64
  434.8 3.8 copy-start.1
  434.8 4.3 copy-start.7
  498.3 148.0 %all-to-all-start.3 = ((bf16[1,32,20,3584]{3,2,0,1:T(8,128)(2,1)}), bf16[1,32,20,3584]{3,2,0,1:T(8,128)(2,1)}, u32[]{:S(2)}, u32[]{:S(2)}) async-start(bf16[1,32,20,3584]{3,2,0,1:T(8,128)(2,1)} %bitcast.389), calls=%async_computation.3 | async-start | bytes 11010048 | tf_op jit(solution)/shard_map/all_to_all | solution.py:64
  503.1 8.2 %copy-start.2 = (bf16[1,64,3584]{2,1,0:T(8,128)(2,1)S(1)}, bf16[1,64,3584]{2,1,0:T(8,128)(2,1)}, u32[]{:S(2)}) copy-start(bf16[1,64,3584]{2,1,0:T(8,128)(2,1)} %param.9) | copy-start | bytes 1376260
  515.0 153.0 %collective-permute-start = (bf16[1,64,3584]{2,1,0:T(8,128)(2,1)}, bf16[1,64,3584]{2,1,0:T(8,128)(2,1)}, u32[]{:S(2)}, u32[]{:S(2)}) collective-permute-start(bf16[1,64,3584]{2,1,0:T(8,128)(2,1)} %fusion.3), channel_id=1, source_target_pairs={{0,32},{32,64},{64,96},{96,128},{128,160},{160,192},{192,224},{224... | collective-permute-start | bytes 1376264 | tf_op jit(solution)/shard_map/ppermute | solution.py:13
  646.3 8.2 %copy-start.3 = (bf16[1,64,3584]{2,1,0:T(8,128)(2,1)S(1)}, bf16[1,64,3584]{2,1,0:T(8,128)(2,1)}, u32[]{:S(2)}) copy-start(bf16[1,64,3584]{2,1,0:T(8,128)(2,1)} %param.15) | copy-start | bytes 1376260
  657.5 25.6 %collective-permute-start.1 = (bf16[1,64,3584]{2,1,0:T(8,128)(2,1)S(1)}, bf16[1,64,3584]{2,1,0:T(8,128)(2,1)S(1)}, u32[]{:S(2)}, u32[]{:S(2)}) collective-permute-start(bf16[1,64,3584]{2,1,0:T(8,128)(2,1)S(1)} %fusion.2), channel_id=1, source_target_pairs={{0,224},{32,0},{64,32},{96,64},{128,96},{160,128},{192,160},{224,1... | collective-permute-start | bytes 1376264 | tf_op jit(solution)/shard_map/ppermute | solution.py:13
